TPU v7x, 256 devices: a whole 4x4x8 slice. The times are simulated.
256 devices in a mesh: mem: 16 (over y_lo, z), lat: 4 (over x), lon: 4 (over y_hi, core).
Axes of the slice: x: 4, y: 4 (y_hi: 2, y_lo: 2; y = y_hi * 2 + y_lo), z: 8, core: 2. Of those that a mesh axis runs over, the one named last changes fastest.
Arguments:
- ensemble: bfloat16 [256, 73, 32, 512], P('mem', None, 'lat', 'lon'), may hold values from -6 to 6
- ancestry: int32 [256], replicated, may hold values from 0 to 255, as said below
- obs_weights: float32 [256], P('mem'), may hold values from 0.1 to 10
- kernel_index: int32 [32], P('lat'), may hold values from 0 to 7
- kernel_table: float32 [8, 9, 73], replicated, may hold values from -3 to 3
- feature_scaling_factor: float32 [73], replicated, may hold values from 0.1 to 1.9
- entry_projection_matrix: bfloat16 [1536, 73], replicated, may hold values from -0.75 to 0.75
- exit_projection_matrix: bfloat16 [73, 1536], replicated, may hold values from -0.15625 to 0.15625
Outputs:
- predicted_particles: bfloat16 [256, 73, 32, 512], P('mem', None, 'lat', 'lon')
- importance_average_state: float32 [73, 32, 512], P(None, 'lat', 'lon')
Inputs may be any that keep to these rules, and one draw needn't show every extreme that they name: `ancestry`: each slot's ancestor member. The slots held by one index of mem take at most 1 distinct ancestors from the members held by any one index of mem.
All inputs are finite; a program needn't handle non-finite values.
Results may differ from a plain program's by a relative error of at most 0.0042.
Values may be sent and summed in bfloat16 or wider, within the bound.
No kernel may reach another device: no remote copies, remote signals or barrier semaphores. Data moves between devices by JAX's collectives and lax.ppermute only.
A program may use at most 128 MiB of HBM per device.

v0:
```python
import jax
import jax.numpy as jnp
from jax import lax
from jax.sharding import PartitionSpec as P

EPS = 1e-06


def extended(block, sides, width, periodic):
    for axis, dim in sides:
        count = lax.axis_size(axis)
        forward = [(i, i + 1) for i in range(count - 1)]
        if periodic:
            forward.append((count - 1, 0))
        backward = [(target, source) for source, target in forward]
        low = lax.ppermute(
            lax.slice_in_dim(block, block.shape[dim] - width, None, axis=dim), axis, forward
        )
        high = lax.ppermute(lax.slice_in_dim(block, 0, width, axis=dim), axis, backward)
        block = jnp.concatenate([low, block, high], axis=dim)
    return block


def finish(conv, field, feature_scaling_factor, entry_projection_matrix, exit_projection_matrix):
    mean_sq = jnp.mean(conv * conv, axis=0)
    normed = (conv * lax.rsqrt(mean_sq + EPS) * feature_scaling_factor[:, None, None]).astype(
        jnp.bfloat16
    )
    flat = normed.reshape(normed.shape[0], -1)
    hidden = jax.nn.gelu(
        jnp.dot(entry_projection_matrix, flat, preferred_element_type=jnp.float32), approximate=True
    ).astype(jnp.bfloat16)
    update = jnp.dot(
        exit_projection_matrix, hidden, preferred_element_type=jnp.float32
    ) + field.reshape(field.shape[0], -1)
    return update.reshape(field.shape).astype(jnp.bfloat16)


def propagate_particles(
    member_tiles,
    filter_coefficients,
    feature_scaling_factor,
    entry_projection_matrix,
    exit_projection_matrix,
):
    widened = extended(member_tiles, (("lat", 2),), 1, False)
    widened = extended(widened, (("lon", 3),), 1, True)

    def one_member(pair):
        particle_state, padded_tile = pair
        field = particle_state.astype(jnp.float32)
        padded = padded_tile.astype(jnp.float32)
        row_count = field.shape[1]
        col_count = field.shape[2]
        conv = jnp.zeros_like(field)
        for tap_index in range(9):
            row_shift = tap_index // 3
            col_shift = tap_index % 3
            conv = (
                conv
                + filter_coefficients[tap_index][:, :, None]
                * padded[:, row_shift : row_shift + row_count, col_shift : col_shift + col_count]
            )
        return finish(
            conv, field, feature_scaling_factor, entry_projection_matrix, exit_projection_matrix
        )

    return lax.map(one_member, (member_tiles, widened))


def replicate_tiles(member_tiles, ancestry):
    my_index = lax.axis_index("mem")
    per_device = member_tiles.shape[0]
    own_parents = lax.dynamic_slice_in_dim(ancestry, my_index * per_device, per_device)
    shard_rows = lax.all_gather(member_tiles, "mem", axis=0, tiled=True)
    row_total = shard_rows.shape[0]
    inside = (own_parents >= 0) & (own_parents < row_total)
    picked = jnp.take(shard_rows, jnp.clip(own_parents, 0, row_total - 1), axis=0)
    return jnp.where(inside[:, None, None, None], picked, jnp.zeros_like(member_tiles))


def shards(
    ensemble,
    ancestry,
    obs_weights,
    kernel_index,
    kernel_table,
    feature_scaling_factor,
    entry_projection_matrix,
    exit_projection_matrix,
):
    kernels = kernel_table.shape[0]
    onehot = (kernel_index[:, None] == jnp.arange(kernels, dtype=jnp.int32)[None, :]).astype(
        jnp.float32
    )
    flat_table = kernel_table.reshape(kernels, -1)
    filter_coefficients = jnp.dot(onehot, flat_table, precision=lax.Precision.HIGHEST)
    filter_coefficients = jnp.transpose(
        filter_coefficients.reshape(kernel_index.shape[0], 9, -1), (1, 2, 0)
    )
    predicted_particles = propagate_particles(
        replicate_tiles(ensemble, ancestry),
        filter_coefficients,
        feature_scaling_factor,
        entry_projection_matrix,
        exit_projection_matrix,
    )

    def accumulate(total, pair):
        weight, particle_state = pair
        return (total + weight * particle_state.astype(jnp.float32), None)

    start_total = jnp.zeros(ensemble.shape[1:], jnp.float32)
    weighted_part, _ = lax.scan(accumulate, start_total, (obs_weights, ensemble))
    importance_aggregate, likelihood_normalizer = lax.psum(
        (weighted_part, jnp.sum(obs_weights)), "mem"
    )
    return (predicted_particles, importance_aggregate / likelihood_normalizer)


def solution(mesh):
    return jax.shard_map(
        shards,
        mesh=mesh,
        in_specs=(P("mem", None, "lat", "lon"), P(), P("mem"), P("lat"), P(), P(), P(), P()),
        out_specs=(P("mem", None, "lat", "lon"), P(None, "lat", "lon")),
        check_vma=False,
    )
```

profile of v0, /device:TPU:2, one launch (start us, length us, event | category | flops | bytes accessed | tf_op | source)
XLA Modules:
  0.0 758.4 jit_solution(7995749304331995080)
XLA Ops:
  8.7 405.1 %all-gather.2.cloned.1.call-done = bf16[256,73,8,128]{3,2,1,0:T(8,128)(2,1)} async-done(((bf16[16,73,8,128]{3,2,1,0:T(8,128)(2,1)}), bf16[256,73,8,128]{3,2,1,0:T(8,128)(2,1)}) %all-gather.2.cloned.1.call-update) | async-done | bytes 38273040 | tf_op jit(solution)/shard_map/all_gather | solution.py:75
  413.9 3.8 gather_fusion
  417.7 2.0 select_select_fusion
  420.6 3.4 collective-permute-start
  424.7 2.5 collective-permute-start.1
  427.2 36.3 %while.24 = (s32[]{:T(128)}, f32[73,8,128]{2,1,0:T(8,128)S(1)}, f32[16]{0:T(128)S(1)}, bf16[16,73,8,128]{3,2,1,0:T(8,128)(2,1)}) while((s32[]{:T(128)}, f32[73,8,128]{2,1,0:T(8,128)S(1)}, f32[16]{0:T(128)S(1)}, bf16[16,73,8,128]{3,2,1,0:T(8,128)(2,1)}) %tuple.76), condition=%wide.region_4.5_spmd.clone.clone, body=%wide.region_3.4_spmd.clone.sunk.clone | while | flops 299011 | bytes 747603 | solution.py:114
  427.8 1.7 bitcast_add_fusion.3
  430.1 1.7 bitcast_add_fusion.3
  432.4 1.7 bitcast_add_fusion.3
  434.6 1.7 bitcast_add_fusion.3
  436.9 1.7 bitcast_add_fusion.3
  439.2 1.7 bitcast_add_fusion.3
  441.4 1.7 bitcast_add_fusion.3
  443.7 1.7 bitcast_add_fusion.3
  446.0 1.7 bitcast_add_fusion.3
  448.3 1.7 bitcast_add_fusion.3
  450.5 1.7 bitcast_add_fusion.3
  452.8 1.7 bitcast_add_fusion.3
  455.1 1.7 bitcast_add_fusion.3
  457.3 1.7 bitcast_add_fusion.3
  459.6 1.7 bitcast_add_fusion.3
  461.9 1.7 bitcast_add_fusion.3
  464.3 32.7 %psum.15 = f32[]{:T(128)} all-reduce(f32[]{:T(128)} %reduce_sum.18), channel_id=1, replica_groups=mesh['mem'=16,'lat'=4,'lon'=4] {'mem'}, use_global_device_ids=true, to_apply=%region_7.8 | all-reduce | flops 1 | bytes 8 | tf_op jit(solution)/shard_map/psum | solution.py:115
  497.9 1.4 copy.44
  500.1 3.3 pad_maximum_fusion.1
  503.4 5.8 fusion.29
  509.2 5.2 copy.45
  514.5 5.1 copy.46
  519.6 3.5 collective-permute-start.3
  523.1 72.4 %all-reduce.2.cloned.1.call-done = f32[73,8,128]{2,1,0:T(8,128)} async-done(((f32[73,8,128]{2,1,0:T(8,128)}), f32[73,8,128]{2,1,0:T(8,128)}) %all-reduce.2.cloned.1.call-update) | async-done | bytes 299024 | tf_op jit(solution)/shard_map/psum | solution.py:115
  595.5 2.3 broadcast_divide_fusion
  597.8 4.3 copy.47
  602.1 4.3 copy.48
  606.3 16.0 %pad_maximum_fusion = bf16[16,73,10,130]{3,2,1,0:T(8,128)(2,1)} fusion(bf16[16,73,10,1]{3,2,1,0:T(8,128)(2,1)} %copy.48, bf16[16,73,1,128]{3,2,1,0:T(2,128)(2,1)} %copy-done.1, bf16[16,73,8,128]{3,2,1,0:T(8,128)(2,1)S(1)} %select_select_fusion, bf16[16,73,1,128]{3,2,1,0:T(2,128)(2,1)S(1)} %copy.43, bf16[16,73,10,1]{3,2,1,0:T(8,128)(2,1)} %copy.47), kind=kLoop, calls=%fused_computation.51 | loop fusion | flops 15184000 | bytes 6073600 | tf_op jit(solution)/shard_map/concatenate | solution.py:20
  622.3 129.2 %while.23 = (s32[]{:T(128)}, bf16[16,73,8,128]{3,2,1,0:T(8,128)(2,1)}, f32[9,73,8]{1,2,0:T(8,128)S(1)}, bf16[16,73,10,130]{3,2,1,0:T(8,128)(2,1)}, f32[73]{0:T(1...) while((s32[]{:T(128)}, ...), condition=%wide.region_2.3_spmd.clone, body=%wide.region_0.2_spmd.sunk.clone | while | flops 475396800 | bytes 8175199 | solution.py:68
  624.4 1.4 multiply_reduce_fusion.3
  626.2 3.5 fusion.45
  632.5 1.4 multiply_reduce_fusion.3
  634.2 3.5 fusion.45
  640.6 1.4 multiply_reduce_fusion.3
  642.3 3.5 fusion.45
  648.7 1.4 multiply_reduce_fusion.3
  650.4 3.5 fusion.45
  656.7 1.4 multiply_reduce_fusion.3
  658.5 3.5 fusion.45
  664.8 1.4 multiply_reduce_fusion.3
  666.5 3.5 fusion.45
  672.9 1.4 multiply_reduce_fusion.3
  674.6 3.5 fusion.45
  681.0 1.4 multiply_reduce_fusion.3
  682.7 3.5 fusion.45
  689.0 1.4 multiply_reduce_fusion.3
  690.8 3.5 fusion.45
  698.8 3.5 fusion.45
  705.2 1.4 multiply_reduce_fusion.3
  706.9 3.5 fusion.45
  715.0 3.5 fusion.45
  721.3 1.4 multiply_reduce_fusion.3
  723.1 3.5 fusion.45
  731.1 3.5 fusion.45
  737.5 1.4 multiply_reduce_fusion.3
  739.2 3.5 fusion.45
  745.6 1.4 multiply_reduce_fusion.3
  747.3 3.5 fusion.45
  (375 shorter events, 69.1 us)
Async XLA Ops:
  7.2 406.7 %all-gather.2.cloned.1.call-start = ((), (), s32[]{:S(2)}) async-start(), calls=%async_computation | async-start | bytes 40665088 | tf_op jit(solution)/shard_map/all_gather | solution.py:75
  7.9 587.6 %all-reduce.2.cloned.1.call-start = ((), (), s32[]{:S(2)}) async-start(), calls=%async_computation.1 | async-start | bytes 598016 | tf_op jit(solution)/shard_map/psum | solution.py:115
  417.7 9.5 %copy-start.6 = (f32[16]{0:T(128)S(1)}, f32[16]{0:T(128)}, u32[]{:S(2)}) copy-start(f32[16]{0:T(128)} %param.14) | copy-start | bytes 196
  419.7 77.2 %copy-start.2 = (f32[8,9,73]{2,0,1:T(8,128)S(1)}, f32[8,9,73]{2,0,1:T(8,128)}, u32[]{:S(2)}) copy-start(f32[8,9,73]{2,0,1:T(8,128)} %param.16) | copy-start | bytes 63076
  419.7 77.4 %copy-start.4 = (s32[8]{0:T(128)S(1)}, s32[8]{0:T(128)}, u32[]{:S(2)}) copy-start(s32[8]{0:T(128)} %param.15) | copy-start | bytes 100
  420.6 76.8 %collective-permute-start = (bf16[16,73,1,128]{3,0,2,1:T(8,128)(2,1)S(1)}, bf16[16,73,1,128]{3,0,2,1:T(8,128)(2,1)S(1)}, u32[]{:S(2)}, u32[]{:S(2)}) collective-permute-start(bf16[16,73,1,128]{3,0,2,1:T(8,128)(2,1)S(1)} %copy.41), channel_id=1, source_target_pairs={{0,4},{4,8},{8,12},{1,5},{5,9},{9,13},{2,6},{6,10},{10,14},{3,7},{... | collective-permute-start | bytes 897032 | tf_op jit(solution)/shard_map/ppermute | solution.py:16
  424.7 73.1 %collective-permute-start.1 = (bf16[16,73,1,128]{3,0,2,1:T(8,128)(2,1)}, bf16[16,73,1,128]{3,0,2,1:T(8,128)(2,1)}, u32[]{:S(2)}, u32[]{:S(2)}) collective-permute-start(bf16[16,73,1,128]{3,0,2,1:T(8,128)(2,1)} %copy.42), channel_id=1, source_target_pairs={{4,0},{8,4},{12,8},{5,1},{9,5},{13,9},{6,2},{10,6},{14,10},{7,3},{... | collective-permute-start | bytes 897032 | tf_op jit(solution)/shard_map/ppermute | solution.py:19
  463.6 0.7 copy-start
  499.3 0.8 copy-start.1
  514.4 83.4 %collective-permute-start.2 = (bf16[16,73,10,1]{1,0,3,2:T(8,128)(2,1)S(1)}, bf16[16,73,10,1]{1,0,3,2:T(8,128)(2,1)S(1)}, u32[]{:S(2)}, u32[]{:S(2)}) collective-permute-start(bf16[16,73,10,1]{1,0,3,2:T(8,128)(2,1)S(1)} %copy.45), channel_id=1, source_target_pairs={{0,1},{1,2},{2,3},{3,0},{4,5},{5,6},{6,7},{7,4},{8,9},{9,10},{10,1... | collective-permute-start | bytes 70088 | tf_op jit(solution)/shard_map/ppermute | solution.py:16
  519.6 82.4 %collective-permute-start.3 = (bf16[16,73,10,1]{1,0,3,2:T(8,128)(2,1)S(1)}, bf16[16,73,10,1]{1,0,3,2:T(8,128)(2,1)S(1)}, u32[]{:S(2)}, u32[]{:S(2)}) collective-permute-start(bf16[16,73,10,1]{1,0,3,2:T(8,128)(2,1)S(1)} %copy.46), channel_id=1, source_target_pairs={{1,0},{2,1},{3,2},{0,3},{5,4},{6,5},{7,6},{4,7},{9,8},{10,9},{11,1... | collective-permute-start | bytes 70088 | tf_op jit(solution)/shard_map/ppermute | solution.py:19
  606.3 16.0 %copy-start.3 = (f32[73]{0:T(128)S(1)}, f32[73]{0:T(128)}, u32[]{:S(2)}) copy-start(f32[73]{0:T(128)} %param.17) | copy-start | bytes 880
  606.3 16.0 %copy-start.5 = (bf16[1536,73]{0,1:T(8,128)(2,1)S(1)}, bf16[1536,73]{0,1:T(8,128)(2,1)}, u32[]{:S(2)}) copy-start(bf16[1536,73]{0,1:T(8,128)(2,1)} %param.18) | copy-start | bytes 672772
Sparse Core Ops, SparseCore 0:
  9.8 404.0 all-gather.1
  464.4 131.0 all-reduce.1
where the time goes:
time: 760 us; the launch traced here: 758 us
  waiting for transfers between devices  478 us (63%)
  other arithmetic  95.7 us (13%)
  local copies, waits for them, and re-layouts  70.1 us (9%)
  matrix products  56.3 us (7%)
  blocking collectives  32.7 us (4%)
  between operations  14.2 us (2%)
  starting transfers between devices  9.5 us (1%)
    all_gather x1, waiting for transfers between devices, replicate_tiles(): shard_rows = lax.all_gather(member_tiles, 'mem', axis=0, tiled=True)  405 us
    psum x1, waiting for transfers between devices, shards(): lax.psum((weighted_part, jnp.sum(obs_weights)), 'mem')  72.4 us
    dot_general x16, matrix products, finish(): jnp.dot(exit_projection_matrix, hidden, preferred_element_type=jnp.float32)  56.1 us
    psum x1, blocking collectives, shards(): lax.psum((weighted_part, jnp.sum(obs_weights)), 'mem')  32.7 us
    add x16, other arithmetic, accumulate(): return (total + weight * particle_state.astype(jnp.float32), None)  26.6 us
    reduce_sum x16, other arithmetic, finish(): mean_sq = jnp.mean(conv * conv, axis=0)  21.8 us
    convert_element_type x16, other arithmetic, one_member(): padded = padded_tile.astype(jnp.float32)  19.4 us
    concatenate x2, other arithmetic, extended(): block = jnp.concatenate([low, block, high], axis=dim)  19.3 us
  transfers between devices with their start and end apart: 6, of which 2 were waited for; matrix products, arithmetic and copies ran while one was open for 9% of the time, Pallas kernels for 0%

commit v1 on v0

--- a/solution.py
+++ b/solution.py
@@ -72,7 +72,9 @@
     my_index = lax.axis_index("mem")
     per_device = member_tiles.shape[0]
     own_parents = lax.dynamic_slice_in_dim(ancestry, my_index * per_device, per_device)
-    shard_rows = lax.all_gather(member_tiles, "mem", axis=0, tiled=True)
+    shard_rows = jnp.concatenate(
+        lax.all_to_all(jnp.stack(lax.axis_size("mem") * [member_tiles]), "mem", 0, 0), axis=0
+    )
     row_total = shard_rows.shape[0]
     inside = (own_parents >= 0) & (own_parents < row_total)
     picked = jnp.take(shard_rows, jnp.clip(own_parents, 0, row_total - 1), axis=0)

time: 760 us -> 1290 us (1.70)
  waiting for transfers between devices: 478 us -> 937 us
  blocking collectives: 32.7 us -> 76.2 us
  local copies, waits for them, and re-layouts: 70.1 us -> 84.1 us
    all_to_all x0 -> x1, waiting for transfers between devices: none -> 863 us  [replicate_tiles(): lax.all_to_all(jnp.stack(lax.axis_size('mem') * [member_tiles]), 'mem', 0...]
    all_gather x1 -> x0, waiting for transfers between devices: 405 us -> none  [replicate_tiles(): shard_rows = lax.all_gather(member_tiles, 'mem', axis=0, tiled=True)]
    psum x1, blocking collectives: 32.7 us -> 76.2 us  [shards(): lax.psum((weighted_part, jnp.sum(obs_weights)), 'mem')]
    another operation x0 -> x1, local copies, waits for them, and re-layouts: none -> 14 us  [replicate_tiles(): jnp.stack(lax.axis_size('mem') * [member_tiles])]
  transfers between devices with their start and end apart: 6 -> 6, of which waited for: 2 -> 2; matrix products, arithmetic and copies ran while one was open for 9% -> 5% of each run, Pallas kernels for 0% -> 0%
where the time goes in v1:
time: 1290 us; the launch traced here: 1280 us
  waiting for transfers between devices  937 us (73%)
  other arithmetic  95 us (7%)
  local copies, waits for them, and re-layouts  84.1 us (7%)
  blocking collectives  76.2 us (6%)
  matrix products  56.2 us (4%)
  starting transfers between devices  19.2 us (1%)
  between operations  14.2 us (1%)
    all_to_all x1, waiting for transfers between devices, replicate_tiles(): lax.all_to_all(jnp.stack(lax.axis_size('mem') * [member_tiles]), 'mem', 0...  863 us
    psum x1, blocking collectives, shards(): lax.psum((weighted_part, jnp.sum(obs_weights)), 'mem')  76.2 us
    psum x1, waiting for transfers between devices, shards(): lax.psum((weighted_part, jnp.sum(obs_weights)), 'mem')  74.2 us
    dot_general x16, matrix products, finish(): jnp.dot(exit_projection_matrix, hidden, preferred_element_type=jnp.float32)  55.9 us
    add x16, other arithmetic, accumulate(): return (total + weight * particle_state.astype(jnp.float32), None)  26.6 us
  transfers between devices with their start and end apart: 6, of which 2 were waited for; matrix products, arithmetic and copies ran while one was open for 5% of the time, Pallas kernels for 0%

profile of v1, /device:TPU:2, one launch (start us, length us, event | category | flops | bytes accessed | tf_op | source)
XLA Modules:
  0.0 1283.8 jit_solution(3802628760393443240)
XLA Ops:
  7.2 14.0 %stack.2 = bf16[16,16,73,8,128]{4,3,2,1,0:T(8,128)(2,1)} broadcast(bf16[16,73,8,128]{3,2,1,0:T(8,128)(2,1)} %param.12), dimensions={1,2,3,4} | broadcast | bytes 40665088 | tf_op jit(solution)/shard_map/stack | solution.py:76
  21.1 9.8 all-to-all-start
  31.1 863.2 %all-to-all-done = bf16[16,16,73,8,128]{4,3,2,1,0:T(8,128)(2,1)} async-done(((bf16[16,16,73,8,128]{4,3,2,1,0:T(8,128)(2,1)}), bf16[16,16,73,8,128]{4,3,2,1,0:T(8,128)(2,1)}, u32[]{:S(2)}, u32[]{:S(2)}) %all-to-all-start) | async-done | bytes 38273056 | tf_op jit(solution)/shard_map/all_to_all | solution.py:76
  894.2 3.8 gather_fusion
  898.0 2.0 select_select_fusion
  900.9 3.4 collective-permute-start
  905.1 2.4 collective-permute-start.1
  907.6 36.3 %while.24 = (s32[]{:T(128)}, f32[73,8,128]{2,1,0:T(8,128)S(1)}, f32[16]{0:T(128)S(1)}, bf16[16,73,8,128]{3,2,1,0:T(8,128)(2,1)}) while((s32[]{:T(128)}, f32[73,8,128]{2,1,0:T(8,128)S(1)}, f32[16]{0:T(128)S(1)}, bf16[16,73,8,128]{3,2,1,0:T(8,128)(2,1)}) %tuple.75), condition=%wide.region_4.5_spmd.clone.clone, body=%wide.region_3.4_spmd.clone.sunk.clone | while | flops 299011 | bytes 747603 | solution.py:116
  908.2 1.7 bitcast_add_fusion.3
  910.5 1.7 bitcast_add_fusion.3
  912.7 1.7 bitcast_add_fusion.3
  915.0 1.7 bitcast_add_fusion.3
  917.3 1.7 bitcast_add_fusion.3
  919.5 1.7 bitcast_add_fusion.3
  921.8 1.7 bitcast_add_fusion.3
  924.1 1.7 bitcast_add_fusion.3
  926.3 1.7 bitcast_add_fusion.3
  928.6 1.7 bitcast_add_fusion.3
  930.9 1.7 bitcast_add_fusion.3
  933.1 1.7 bitcast_add_fusion.3
  935.4 1.7 bitcast_add_fusion.3
  937.7 1.7 bitcast_add_fusion.3
  940.0 1.7 bitcast_add_fusion.3
  942.2 1.7 bitcast_add_fusion.3
  944.6 76.2 %psum.15 = f32[]{:T(128)} all-reduce(f32[]{:T(128)} %reduce_sum.18), channel_id=1, replica_groups=mesh['mem'=16,'lat'=4,'lon'=4] {'mem'}, use_global_device_ids=true, to_apply=%region_7.8 | all-reduce | flops 1 | bytes 8 | tf_op jit(solution)/shard_map/psum | solution.py:117
  1021.7 1.4 copy.62
  1024.0 3.3 pad_maximum_fusion.1
  1027.2 5.8 fusion.29
  1033.0 5.1 copy.63
  1038.3 5.2 copy.64
  1043.5 3.5 collective-permute-start.3
  1046.9 74.2 %all-reduce.2.cloned.1.call-done = f32[73,8,128]{2,1,0:T(8,128)} async-done(((f32[73,8,128]{2,1,0:T(8,128)}), f32[73,8,128]{2,1,0:T(8,128)}) %all-reduce.2.cloned.1.call-update) | async-done | bytes 299024 | tf_op jit(solution)/shard_map/psum | solution.py:117
  1121.1 2.3 broadcast_divide_fusion
  1123.4 4.3 copy.65
  1127.6 4.3 copy.66
  1131.9 16.0 %pad_maximum_fusion = bf16[16,73,10,130]{3,2,1,0:T(8,128)(2,1)} fusion(bf16[16,73,10,1]{3,2,1,0:T(8,128)(2,1)} %copy.66, bf16[16,73,1,128]{3,2,1,0:T(2,128)(2,1)} %copy-done.1, bf16[16,73,8,128]{3,2,1,0:T(8,128)(2,1)S(1)} %select_select_fusion, bf16[16,73,1,128]{3,2,1,0:T(2,128)(2,1)S(1)} %copy.61, bf16[16,73,10,1]{3,2,1,0:T(8,128)(2,1)} %copy.65), kind=kLoop, calls=%fused_computation.51 | loop fusion | flops 15184000 | bytes 6073600 | tf_op jit(solution)/shard_map/concatenate | solution.py:20
  1147.9 129.1 %while.23 = (s32[]{:T(128)}, bf16[16,73,8,128]{3,2,1,0:T(8,128)(2,1)}, f32[9,73,8]{1,2,0:T(8,128)S(1)}, bf16[16,73,10,130]{3,2,1,0:T(8,128)(2,1)}, f32[73]{0:T(1...) while((s32[]{:T(128)}, ...), condition=%wide.region_2.3_spmd.clone, body=%wide.region_0.2_spmd.sunk.clone | while | flops 475396800 | bytes 8175199 | solution.py:68
  1150.0 1.4 multiply_reduce_fusion.3
  1151.7 3.5 fusion.45
  1158.1 1.4 multiply_reduce_fusion.3
  1159.8 3.5 fusion.45
  1166.2 1.4 multiply_reduce_fusion.3
  1167.9 3.5 fusion.45
  1174.2 1.4 multiply_reduce_fusion.3
  1176.0 3.5 fusion.45
  1182.3 1.4 multiply_reduce_fusion.3
  1184.0 3.5 fusion.45
  1190.4 1.4 multiply_reduce_fusion.3
  1192.1 3.5 fusion.45
  1198.4 1.4 multiply_reduce_fusion.3
  1200.2 3.5 fusion.45
  1206.5 1.4 multiply_reduce_fusion.3
  1208.2 3.5 fusion.45
  1216.3 3.5 fusion.45
  1222.6 1.4 multiply_reduce_fusion.3
  1224.4 3.5 fusion.45
  1232.4 3.5 fusion.45
  1240.5 3.5 fusion.45
  1246.8 1.4 multiply_reduce_fusion.3
  1248.6 3.5 fusion.45
  1256.6 3.5 fusion.45
  1263.0 1.4 multiply_reduce_fusion.3
  1264.7 3.5 fusion.45
  1272.8 3.5 fusion.45
  (377 shorter events, 70.5 us)
Async XLA Ops:
  21.1 9.8 copy-start.5
  21.1 873.1 %all-to-all-start = ((bf16[16,16,73,8,128]{4,3,2,1,0:T(8,128)(2,1)}), bf16[16,16,73,8,128]{4,3,2,1,0:T(8,128)(2,1)}, u32[]{:S(2)}, u32[]{:S(2)}) async-start(bf16[16,16,73,8,128]{4,3,2,1,0:T(8,128)(2,1)} %stack.2), calls=%async_computation | async-start | bytes 76546048 | tf_op jit(solution)/shard_map/all_to_all | solution.py:76
  30.9 1090.2 %all-reduce.2.cloned.1.call-start = ((), (), s32[]{:S(2)}) async-start(), calls=%async_computation.1 | async-start | bytes 598016 | tf_op jit(solution)/shard_map/psum | solution.py:117
  898.0 9.5 copy-start.7
  900.1 120.7 %copy-start.2 = (f32[8,9,73]{2,0,1:T(8,128)S(1)}, f32[8,9,73]{2,0,1:T(8,128)}, u32[]{:S(2)}) copy-start(f32[8,9,73]{2,0,1:T(8,128)} %param.16) | copy-start | bytes 63076
  900.1 120.9 %copy-start.4 = (s32[8]{0:T(128)S(1)}, s32[8]{0:T(128)}, u32[]{:S(2)}) copy-start(s32[8]{0:T(128)} %param.15) | copy-start | bytes 100
  900.9 120.3 %collective-permute-start = (bf16[16,73,1,128]{3,0,2,1:T(8,128)(2,1)S(1)}, bf16[16,73,1,128]{3,0,2,1:T(8,128)(2,1)S(1)}, u32[]{:S(2)}, u32[]{:S(2)}) collective-permute-start(bf16[16,73,1,128]{3,0,2,1:T(8,128)(2,1)S(1)} %copy.59), channel_id=1, source_target_pairs={{0,4},{4,8},{8,12},{1,5},{5,9},{9,13},{2,6},{6,10},{10,14},{3,7},{... | collective-permute-start | bytes 897032 | tf_op jit(solution)/shard_map/ppermute | solution.py:16
  905.1 116.6 %collective-permute-start.1 = (bf16[16,73,1,128]{3,0,2,1:T(8,128)(2,1)}, bf16[16,73,1,128]{3,0,2,1:T(8,128)(2,1)}, u32[]{:S(2)}, u32[]{:S(2)}) collective-permute-start(bf16[16,73,1,128]{3,0,2,1:T(8,128)(2,1)} %copy.60), channel_id=1, source_target_pairs={{4,0},{8,4},{12,8},{5,1},{9,5},{13,9},{6,2},{10,6},{14,10},{7,3},{... | collective-permute-start | bytes 897032 | tf_op jit(solution)/shard_map/ppermute | solution.py:19
  943.9 0.7 copy-start
  1023.1 0.8 copy-start.1
  1038.2 85.2 %collective-permute-start.2 = (bf16[16,73,10,1]{1,0,3,2:T(8,128)(2,1)S(1)}, bf16[16,73,10,1]{1,0,3,2:T(8,128)(2,1)S(1)}, u32[]{:S(2)}, u32[]{:S(2)}) collective-permute-start(bf16[16,73,10,1]{1,0,3,2:T(8,128)(2,1)S(1)} %copy.63), channel_id=1, source_target_pairs={{0,1},{1,2},{2,3},{3,0},{4,5},{5,6},{6,7},{7,4},{8,9},{9,10},{10,1... | collective-permute-start | bytes 70088 | tf_op jit(solution)/shard_map/ppermute | solution.py:16
  1043.5 84.2 %collective-permute-start.3 = (bf16[16,73,10,1]{1,0,3,2:T(8,128)(2,1)S(1)}, bf16[16,73,10,1]{1,0,3,2:T(8,128)(2,1)S(1)}, u32[]{:S(2)}, u32[]{:S(2)}) collective-permute-start(bf16[16,73,10,1]{1,0,3,2:T(8,128)(2,1)S(1)} %copy.64), channel_id=1, source_target_pairs={{1,0},{2,1},{3,2},{0,3},{5,4},{6,5},{7,6},{4,7},{9,8},{10,9},{11,1... | collective-permute-start | bytes 70088 | tf_op jit(solution)/shard_map/ppermute | solution.py:19
  1131.9 16.0 %copy-start.3 = (f32[73]{0:T(128)S(1)}, f32[73]{0:T(128)}, u32[]{:S(2)}) copy-start(f32[73]{0:T(128)} %param.17) | copy-start | bytes 880
  1131.9 16.0 %copy-start.6 = (bf16[1536,73]{0,1:T(8,128)(2,1)S(1)}, bf16[1536,73]{0,1:T(8,128)(2,1)}, u32[]{:S(2)}) copy-start(bf16[1536,73]{0,1:T(8,128)(2,1)} %param.18) | copy-start | bytes 672772
Sparse Core Ops, SparseCore 0:
  944.8 176.3 all-reduce.1
